TPU v7x, 128 devices: a whole 4x4x4 slice. The times are simulated.
128 devices in a mesh: stn: 8 (over x_hi, y), tm: 16 (over x_lo, z, core).
Axes of the slice: x: 4 (x_hi: 2, x_lo: 2; x = x_hi * 2 + x_lo), y: 4, z: 4, core: 2. Of those that a mesh axis runs over, the one named last changes fastest.
Arguments:
- voltages: bfloat16 [512, 256, 4096], P('stn', 'tm'), may hold values from -52 to 52
- pfb_taps: float32 [16, 4096], replicated, may hold values from -1.5 to 1.5
- eq_gains: float32 [512, 2048], P('stn'), may hold values from 0.5 to 11
Outputs:
- visibilities: float32 [2048, 512, 512], P(('stn', 'tm'))
All inputs are finite; a program needn't handle non-finite values.
Results may differ from a plain program's by a relative error of at most 0.0014.
Values may be sent and summed in bfloat16 or wider, within the bound.
No kernel may reach another device: no remote copies, remote signals or barrier semaphores. Data moves between devices by JAX's collectives and lax.ppermute only.
A program may use at most 448 MiB of HBM per device.

v0:
```python
import math
import jax
import jax.numpy as jnp
from jax import lax
from jax.sharding import PartitionSpec as P


def from_behind(value, axis, steps):
    count = lax.axis_size(axis)
    first, last = (max(0, -steps), min(count, count - steps))
    return lax.ppermute(value, axis, [(source, source + steps) for source in range(first, last)])


def cos_sin(numer, denom):
    angle = 2.0 * math.pi / denom * (numer % denom).astype(jnp.float32)
    return (jnp.cos(angle), jnp.sin(angle))


def transform(filtered, channels):
    inputs_dev, frames_dev, length = filtered.shape
    inner_len = 64
    outer_len = length // inner_len
    kept_upper = channels // outer_len
    row_count = inputs_dev * frames_dev
    highest = lax.Precision.HIGHEST
    arranged = filtered.reshape(row_count, outer_len, inner_len)
    freq_one = lax.broadcasted_iota(jnp.int32, (outer_len, outer_len), 0)
    time_one = lax.broadcasted_iota(jnp.int32, (outer_len, outer_len), 1)
    cos_one, sin_one = cos_sin(freq_one * time_one, outer_len)
    section_one = jnp.stack([cos_one, -sin_one])
    partial_ft = jnp.einsum("qka,Rab->qkbR", section_one, arranged, precision=highest)
    freq_twist = lax.broadcasted_iota(jnp.int32, (outer_len, inner_len), 0)
    time_twist = lax.broadcasted_iota(jnp.int32, (outer_len, inner_len), 1)
    twist_cos, twist_sin = cos_sin(freq_twist * time_twist, length)
    twist_table = jnp.stack([jnp.stack([twist_cos, twist_sin]), jnp.stack([-twist_sin, twist_cos])])
    freq_two = lax.broadcasted_iota(jnp.int32, (kept_upper, inner_len), 0)
    time_two = lax.broadcasted_iota(jnp.int32, (kept_upper, inner_len), 1)
    cos_two, sin_two = cos_sin(freq_two * time_two, inner_len)
    section_two = jnp.stack(
        [jnp.stack([cos_two, sin_two], axis=1), jnp.stack([-sin_two, cos_two], axis=1)]
    )
    combined = jnp.einsum("qjrb,rskb->qjksb", section_two, twist_table, precision=highest)
    spectrum = jnp.einsum("qjksb,skbR->qjkR", combined, partial_ft, precision=highest)
    return spectrum.reshape(2, channels, row_count)


def per_device(voltages, pfb_taps, eq_gains):
    tap_count = pfb_taps.shape[0]
    history_len = tap_count - 1
    inputs_dev, frames_dev, length = voltages.shape
    channels = eq_gains.shape[1]
    station_groups = lax.axis_size("stn")
    time_groups = lax.axis_size("tm")
    per_group = channels // (station_groups * time_groups)
    all_inputs = inputs_dev * station_groups
    all_frames = frames_dev * time_groups
    earlier = from_behind(voltages[:, frames_dev - history_len :, :], "tm", 1)
    extended = jnp.concatenate([earlier, voltages], axis=1).astype(jnp.float32)
    kernel = jnp.flip(pfb_taps, axis=0)[:, None, :]
    filtered = lax.conv_general_dilated(
        extended,
        kernel,
        (1,),
        "VALID",
        dimension_numbers=("NWC", "WIO", "NWC"),
        feature_group_count=length,
        precision=lax.Precision.HIGHEST,
    )
    spectrum = transform(filtered, channels)
    gains_turned = jnp.transpose(eq_gains)
    spectra = (
        spectrum.reshape(2, channels, inputs_dev, frames_dev) * gains_turned[None, :, :, None]
    ).astype(jnp.bfloat16)
    shaped = spectra.reshape(2, station_groups * time_groups, per_group, inputs_dev * frames_dev)
    turned = lax.all_to_all(shaped, ("stn", "tm"), split_axis=1, concat_axis=1, tiled=True)
    blocks = turned.reshape(2, station_groups, time_groups, per_group, inputs_dev, frames_dev)
    columns = jnp.transpose(blocks, (0, 3, 1, 4, 2, 5)).reshape(
        2, per_group, all_inputs, all_frames
    )
    swapped = jnp.stack([columns[1], -columns[0]])
    vis_real = jnp.einsum("rcnt,rcmt->cnm", columns, columns, preferred_element_type=jnp.float32)
    vis_imag = jnp.einsum("rcnt,rcmt->cnm", swapped, columns, preferred_element_type=jnp.float32)
    local_power = jnp.sum(jnp.diagonal(vis_real, axis1=1, axis2=2), axis=0)
    power = lax.psum(local_power, ("stn", "tm"))
    scale = lax.rsqrt(power / (all_frames * channels) + 1e-06)
    weight = scale[:, None] * scale[None, :] / all_frames
    row_ids = lax.broadcasted_iota(jnp.int32, (all_inputs, all_inputs), 0)
    col_ids = lax.broadcasted_iota(jnp.int32, (all_inputs, all_inputs), 1)
    lower = row_ids >= col_ids
    return jnp.where(lower[None], vis_real, vis_imag) * weight[None]


def solution(mesh):
    in_specs = (P("stn", "tm", None), P(), P("stn", None))
    out_specs = P(("stn", "tm"), None, None)
    return jax.shard_map(
        per_device, mesh=mesh, in_specs=in_specs, out_specs=out_specs, check_vma=False
    )
```

profile of v0, /device:TPU:1, one launch (start us, length us, event | category | flops | bytes accessed | tf_op | source)
XLA Modules:
  0.0 891.8 jit_solution(8095447733145545676)
XLA Ops:
  0.0 11.4 %copy.46 = bf16[64,16,4096]{2,0,1:T(8,128)(2,1)} copy(bf16[64,16,4096]{2,1,0:T(8,128)(2,1)} %param.3) | data formatting | bytes 16777216 | tf_op args[0]
  11.4 7.4 slice.19
  24.7 5.3 convolution_bitcast_fusion.2
  29.9 6.8 copy.54
  37.6 21.5 %mul.180 = f32[2048,64,16]{2,1,0:T(8,128)} broadcast(f32[2048,64]{1,0:T(8,128)S(1)} %copy.56), dimensions={0,1} | broadcast | bytes 8912896 | tf_op jit(solution)/shard_map/mul | solution.py:72
  59.0 54.5 %mul.181 = f32[128,16,1024]{2,1,0:T(8,128)} reshape(f32[2048,64,16]{2,1,0:T(8,128)} %mul.180) | data formatting | bytes 16777216 | tf_op jit(solution)/shard_map/mul | solution.py:72
  114.3 22.0 %fusion.3 = f32[64,16,4096]{2,0,1:T(8,128)S(1)} fusion(bf16[64,16,4096]{2,0,1:T(8,128)(2,1)} %copy.46, bf16[64,15,4096]{2,0,1:T(8,128)(2,1)} %collective-permute-done, f32[16,1,4096]{2,0,1:T(8,128)S(1)} %bitcast.69), kind=kOutput, calls=%fused_computation.6 | convolution fusion | flops 813432832 | bytes 33292288 | tf_op jit(solution)/shard_map/conv_general_dilated | solution.py:60
  136.4 18.8 %copy.49 = f32[64,16,4096]{2,1,0:T(8,128)} copy(f32[64,16,4096]{2,0,1:T(8,128)S(1)} %fusion.3) | data formatting | bytes 33554432 | tf_op jit(solution)/shard_map/conv_general_dilated | solution.py:60
  155.2 27.0 %reshape.234 = f32[1024,64,64]{2,1,0:T(8,128)} reshape(f32[64,16,4096]{2,1,0:T(8,128)} %copy.49) | data formatting | bytes 33554432 | tf_op jit(solution)/shard_map/reshape | solution.py:26
  182.2 26.2 %copy.69 = f32[1024,64,64,1]{0,1,3,2:T(8,128)} copy(f32[1024,64,64,1]{2,1,0,3:T(8,128)} %bitcast.62) | data formatting | bytes 33554432 | tf_op jit(solution)/shard_map/reshape | solution.py:26
  208.4 33.7 %convolution_bitcast_fusion = f32[2,64,64,1024,1]{3,1,0,2,4:T(8,128)} fusion(f32[1024,64,64,1]{0,1,3,2:T(8,128)} %copy.69, f32[1,64,64]{2,1,0:T(8,128)S(1)} %copy-done.5, f32[1,64,64]{2,1,0:T(8,128)S(1)} %copy-done.6), kind=kOutput, calls=%fused_computation.10 | convolution fusion | flops 6442459136 | bytes 50364416 | tf_op jit(solution)/shard_map/qka,Rab->qkbR/dot_general | solution.py:31
  242.1 47.6 %fusion.7 = f32[2,32,64,1024]{3,1,0,2:T(8,128)} fusion(f32[2,32,64,2,64]{4,1,3,0,2:T(8,128)S(1)} %copy-done.1, f32[2,64,64,1024,1]{3,1,0,2,4:T(8,128)} %convolution_bitcast_fusion), kind=kOutput, calls=%fused_computation.11 | convolution fusion | flops 6442450944 | bytes 52428800 | tf_op jit(solution)/shard_map/qjksb,skbR->qjkR/dot_general | solution.py:43
  289.7 15.6 %copy.55 = f32[2,32,64,1024]{3,2,1,0:T(8,128)S(1)} copy(f32[2,32,64,1024]{3,1,0,2:T(8,128)} %fusion.7) | data formatting | bytes 33554432 | tf_op jit(solution)/shard_map/qjksb,skbR->qjkR/transpose | solution.py:43
  310.5 8.5 copy.57
  319.0 10.1 %all-to-all-start = ((bf16[2,128,16,1024]{3,2,0,1:T(8,128)(2,1)}), bf16[2,128,16,1024]{3,2,0,1:T(8,128)(2,1)}, u32[]{:S(2)}, u32[]{:S(2)}) async-start(bf16[2,128,16,1024]{3,2,0,1:T(8,128)(2,1)} %copy.57), calls=%async_computation | async-start | bytes 16777216 | tf_op jit(solution)/shard_map/all_to_all | solution.py:75
  330.4 100.1 %all-to-all-done = bf16[2,128,16,1024]{3,2,0,1:T(8,128)(2,1)} async-done(((bf16[2,128,16,1024]{3,2,0,1:T(8,128)(2,1)}), bf16[2,128,16,1024]{3,2,0,1:T(8,128)(2,1)}, u32[]{:S(2)}, u32[]{:S(2)}) %all-to-all-start) | async-done | bytes 8388640 | tf_op jit(solution)/shard_map/all_to_all | solution.py:75
  430.5 62.1 %reshape.251 = bf16[2,8,16,16,64,16]{5,4,3,0,2,1:T(8,128)(2,1)} reshape(bf16[2,128,16,1024]{3,2,0,1:T(8,128)(2,1)} %all-to-all-done) | data formatting | bytes 16777216 | tf_op jit(solution)/shard_map/reshape | solution.py:76
  492.6 56.9 %copy.59 = bf16[2,8,16,16,64,16]{4,5,2,1,3,0:T(8,128)(2,1)} copy(bf16[2,8,16,16,64,16]{5,4,3,0,2,1:T(8,128)(2,1)} %reshape.251) | data formatting | bytes 16777216 | tf_op jit(solution)/shard_map/reshape | solution.py:76
  549.5 57.9 %copy.60 = bf16[2,16,8,64,16,16]{3,2,5,4,1,0:T(8,128)(2,1)} copy(bf16[2,16,8,64,16,16]{5,3,1,0,4,2:T(8,128)(2,1)} %bitcast.18) | data formatting | bytes 16777216 | tf_op jit(solution)/shard_map/transpose | solution.py:77
  607.4 22.5 %reshape.236 = bf16[2,16,512,256]{2,3,1,0:T(8,128)(2,1)} reshape(bf16[2,16,8,64,16,16]{3,2,5,4,1,0:T(8,128)(2,1)} %copy.60) | data formatting | bytes 16777216 | tf_op jit(solution)/shard_map/reshape | solution.py:77
  629.9 16.5 %convolution_bitcast_fusion.1 = f32[16,512,512]{2,1,0:T(8,128)} fusion(bf16[2,16,512,256]{2,3,1,0:T(8,128)(2,1)} %reshape.236), kind=kOutput, calls=%fused_computation.12 | convolution fusion | flops 4294967296 | bytes 25165824 | tf_op jit(solution)/shard_map/rcnt,rcmt->cnm/dot_general | solution.py:81
  646.3 11.7 %fusion.44 = (bf16[1,16,8,64,16,16]{3,5,4,2,1,0:T(8,128)(2,1)}, bf16[1,16,8,64,16,16]{3,5,4,2,1,0:T(8,128)(2,1)}) fusion(bf16[2,16,8,64,16,16]{3,5,4,2,1,0:T(8,128)(2,1)} %bitcast.63), kind=kLoop, calls=%fused_computation.70 | loop fusion | flops 2097152 | bytes 16777216 | tf_op jit(solution)/shard_map/slice | solution.py:80
  658.0 20.2 %copy.64 = bf16[1,16,8,64,16,16]{3,2,5,4,1,0:T(8,128)(2,1)} copy(bf16[1,16,8,64,16,16]{3,5,4,2,1,0:T(8,128)(2,1)} %get-tuple-element.6) | data formatting | bytes 8388608 | tf_op jit(solution)/shard_map/neg | solution.py:80
  678.2 11.8 %neg.47 = bf16[1,16,512,256]{2,3,1,0:T(8,128)(2,1)} reshape(bf16[1,16,8,64,16,16]{3,2,5,4,1,0:T(8,128)(2,1)} %copy.64) | data formatting | bytes 8388608 | tf_op jit(solution)/shard_map/neg | solution.py:80
  690.1 6.3 copy.66
  696.4 20.2 %copy.63 = bf16[1,16,8,64,16,16]{3,2,5,4,1,0:T(8,128)(2,1)} copy(bf16[1,16,8,64,16,16]{3,5,4,2,1,0:T(8,128)(2,1)} %get-tuple-element.5) | data formatting | bytes 8388608 | tf_op jit(solution)/shard_map/slice | solution.py:80
  716.6 11.8 %slice.15 = bf16[1,16,512,256]{2,3,1,0:T(8,128)(2,1)} reshape(bf16[1,16,8,64,16,16]{3,2,5,4,1,0:T(8,128)(2,1)} %copy.63) | data formatting | bytes 8388608 | tf_op jit(solution)/shard_map/slice | solution.py:80
  728.4 6.3 copy.65
  734.8 62.4 %copy.68 = f32[16,512,512]{0,2,1:T(8,128)} copy(f32[16,512,512]{2,1,0:T(8,128)} %convolution_bitcast_fusion.1) | data formatting | bytes 33554432 | tf_op jit(solution)/shard_map/rcnt,rcmt->cnm/dot_general | solution.py:81
  797.1 5.5 gather_fusion
  802.8 69.5 %psum.7 = f32[512]{0:T(512)S(1)} all-reduce(f32[512]{0:T(512)S(1)} %reduce_sum.9), channel_id=1, replica_groups=mesh['stn'=8,'tm'=16] {'stn','tm'}, use_global_device_ids=true, to_apply=%region_1.2 | all-reduce | flops 512 | bytes 4096 | tf_op jit(solution)/shard_map/psum | solution.py:84
  872.5 18.9 %fusion.2 = f32[16,512,512]{2,1,0:T(8,128)} fusion(f32[16,512,512]{2,1,0:T(8,128)} %convolution_bitcast_fusion.1, bf16[1,16,512,256]{3,2,0,1:T(8,128)(2,1)} %copy.66, bf16[1,16,512,256]{3,2,0,1:T(8,128)(2,1)} %copy.65, bf16[2,16,512,256]{2,3,1,0:T(8,128)(2,1)} %reshape.236, f32[512,512]{1,0:T(8,128)S(1)} %multiply_multiply_fusion, ...), kind=kOutput, calls=%fused_computation.4 | convolution fusion | flops 4307550208 | bytes 51642368 | tf_op jit(solution)/shard_map/rcnt,rcmt->cnm/dot_general | solution.py:82
  (40 shorter events, 14.2 us)
Async XLA Ops:
  18.8 18.0 %copy-start.4 = (f32[16,4096]{1,0:T(8,128)S(1)}, f32[16,4096]{1,0:T(8,128)}, u32[]{:S(2)}) copy-start(f32[16,4096]{1,0:T(8,128)} %param.4) | copy-start | bytes 786436
  18.8 18.5 %copy-start.3 = (f32[64,2048]{1,0:T(8,128)S(1)}, f32[64,2048]{1,0:T(8,128)}, u32[]{:S(2)}) copy-start(f32[64,2048]{1,0:T(8,128)} %param.5) | copy-start | bytes 1572868
  18.8 95.6 %collective-permute-start = (bf16[64,15,4096]{2,0,1:T(8,128)(2,1)}, bf16[64,15,4096]{2,0,1:T(8,128)(2,1)}, u32[]{:S(2)}, u32[]{:S(2)}) collective-permute-start(bf16[64,15,4096]{2,0,1:T(8,128)(2,1)} %slice.19), channel_id=1, source_target_pairs={{0,1},{1,2},{2,3},{3,4},{4,5},{5,6},{6,7},{7,8},{8,9},{9,10},{10,1... | collective-permute-start | bytes 23592968 | tf_op jit(solution)/shard_map/ppermute | solution.py:11
  182.2 26.2 %copy-start.5 = (f32[1,64,64]{2,1,0:T(8,128)S(1)}, f32[1,64,64]{2,1,0:T(8,128)}, u32[]{:S(2)}) copy-start(f32[1,64,64]{2,1,0:T(8,128)} %get-tuple-element.15) | copy-start | bytes 49156
  182.2 26.2 %copy-start.6 = (f32[1,64,64]{2,1,0:T(8,128)S(1)}, f32[1,64,64]{2,1,0:T(8,128)}, u32[]{:S(2)}) copy-start(f32[1,64,64]{2,1,0:T(8,128)} %get-tuple-element.16) | copy-start | bytes 49156
  208.4 33.7 %copy-start.1 = (f32[2,32,64,2,64]{4,1,3,0,2:T(8,128)S(1)}, f32[2,32,64,2,64]{4,1,3,0,2:T(8,128)}, u32[]{:S(2)}) copy-start(f32[2,32,64,2,64]{4,1,3,0,2:T(8,128)} %copy.54) | copy-start | bytes 6291460
  208.4 96.9 %slice-start = ((s8[8388608]{0:T(1024)(128)(4,1)}), s8[4194304]{0:T(1024)(128)(4,1)S(1)}, s32[]{:S(2)}) async-start(s8[8388608]{0:T(1024)(128)(4,1)} %bitcast.66), calls=%async_computation.1 | async-start | bytes 8388608
  242.1 63.2 %slice-start.1 = ((s8[8388608]{0:T(1024)(128)(4,1)}), s8[4194304]{0:T(1024)(128)(4,1)S(1)}, s32[]{:S(2)}) async-start(s8[8388608]{0:T(1024)(128)(4,1)} %bitcast.66), calls=%async_computation.2 | async-start | bytes 8388608
  319.0 111.6 %all-to-all-start = ((bf16[2,128,16,1024]{3,2,0,1:T(8,128)(2,1)}), bf16[2,128,16,1024]{3,2,0,1:T(8,128)(2,1)}, u32[]{:S(2)}, u32[]{:S(2)}) async-start(bf16[2,128,16,1024]{3,2,0,1:T(8,128)(2,1)} %copy.57), calls=%async_computation | async-start | bytes 16777216 | tf_op jit(solution)/shard_map/all_to_all | solution.py:75
  734.8 62.4 %copy-start = (s32[512,1]{0,1:T(1,128)S(1)}, s32[512,1]{0,1:T(1,128)}, u32[]{:S(2)}) copy-start(s32[512,1]{0,1:T(1,128)} %shift-left_or_fusion) | copy-start | bytes 6148
  734.8 137.7 %copy-start.2 = (pred[512,512]{1,0:T(8,128)(4,1)S(1)}, pred[512,512]{1,0:T(8,128)(4,1)}, u32[]{:S(2)}) copy-start(pred[512,512]{1,0:T(8,128)(4,1)} %iota_compare_fusion) | copy-start | bytes 786436
where the time goes:
time: 907 us; the launch traced here: 892 us
  local copies, waits for them, and re-layouts  543 us (60%)
  matrix products  144 us (16%)
  waiting for transfers between devices  100 us (11%)
  blocking collectives  69.5 us (8%)
  other arithmetic  19.7 us (2%)
  starting transfers between devices  15.2 us (2%)
    reshape x2, local copies, waits for them, and re-layouts, per_device(): turned.reshape(2, station_groups, time_groups, per_group, inputs_dev, fra...  119 us
    all_to_all x1, waiting for transfers between devices, per_device(): lax.all_to_all(shaped, ('stn', 'tm'), split_axis=1, concat_axis=1, tiled=...  100 us
    mul x2, local copies, waits for them, and re-layouts, per_device(): spectrum.reshape(2, channels, inputs_dev, frames_dev)  76 us
    psum x1, blocking collectives, per_device(): power = lax.psum(local_power, ('stn', 'tm'))  69.5 us
    dot_general x1, local copies, waits for them, and re-layouts, per_device(): jnp.einsum('rcnt,rcmt->cnm', columns, columns, preferred_element_type=jnp...  62.4 us
    transpose x1, local copies, waits for them, and re-layouts, per_device(): jnp.transpose(blocks, (0, 3, 1, 4, 2, 5))  57.9 us
    reshape x2, local copies, waits for them, and re-layouts, transform(): arranged = filtered.reshape(row_count, outer_len, inner_len)  53.2 us
    dot_general x1, matrix products, transform(): jnp.einsum('qjksb,skbR->qjkR', combined, partial_ft, precision=highest)  47.6 us
  transfers between devices with their start and end apart: 2, of which 1 were waited for; matrix products, arithmetic and copies ran while one was open for 10% of the time, Pallas kernels for 0%

commit v1 on v0

--- a/solution.py
+++ b/solution.py
@@ -81,7 +81,7 @@
     vis_real = jnp.einsum("rcnt,rcmt->cnm", columns, columns, preferred_element_type=jnp.float32)
     vis_imag = jnp.einsum("rcnt,rcmt->cnm", swapped, columns, preferred_element_type=jnp.float32)
     local_power = jnp.sum(jnp.diagonal(vis_real, axis1=1, axis2=2), axis=0)
-    power = lax.psum(local_power, ("stn", "tm"))
+    power = lax.psum(lax.psum(local_power, "stn"), "tm")
     scale = lax.rsqrt(power / (all_frames * channels) + 1e-06)
     weight = scale[:, None] * scale[None, :] / all_frames
     row_ids = lax.broadcasted_iota(jnp.int32, (all_inputs, all_inputs), 0)

time: 907 us -> 889 us (0.980)
  blocking collectives: 69.5 us -> 51.9 us
    psum x1 -> x2, blocking collectives: 69.5 us -> 51.9 us  [per_device(): power = lax.psum(lax.psum(local_power, 'stn'), 'tm')]
  transfers between devices with their start and end apart: 2 -> 2, of which waited for: 1 -> 1; matrix products, arithmetic and copies ran while one was open for 10% -> 11% of each run, Pallas kernels for 0% -> 0%
where the time goes in v1:
time: 889 us; the launch traced here: 874 us
  local copies, waits for them, and re-layouts  542 us (61%)
  matrix products  144 us (16%)
  waiting for transfers between devices  100 us (11%)
  blocking collectives  51.9 us (6%)
  other arithmetic  19.8 us (2%)
  starting transfers between devices  15.2 us (2%)
    reshape x2, local copies, waits for them, and re-layouts, per_device(): turned.reshape(2, station_groups, time_groups, per_group, inputs_dev, fra...  119 us
    all_to_all x1, waiting for transfers between devices, per_device(): lax.all_to_all(shaped, ('stn', 'tm'), split_axis=1, concat_axis=1, tiled=...  100 us
    mul x2, local copies, waits for them, and re-layouts, per_device(): spectrum.reshape(2, channels, inputs_dev, frames_dev)  76 us
    dot_general x1, local copies, waits for them, and re-layouts, per_device(): jnp.einsum('rcnt,rcmt->cnm', columns, columns, preferred_element_type=jnp...  61.6 us
    transpose x1, local copies, waits for them, and re-layouts, per_device(): jnp.transpose(blocks, (0, 3, 1, 4, 2, 5))  57.9 us
    reshape x2, local copies, waits for them, and re-layouts, transform(): arranged = filtered.reshape(row_count, outer_len, inner_len)  53.3 us
    psum x2, blocking collectives, per_device(): power = lax.psum(lax.psum(local_power, 'stn'), 'tm')  51.9 us
    dot_general x1, matrix products, transform(): jnp.einsum('qjksb,skbR->qjkR', combined, partial_ft, precision=highest)  47.6 us
  transfers between devices with their start and end apart: 2, of which 1 were waited for; matrix products, arithmetic and copies ran while one was open for 11% of the time, Pallas kernels for 0%

profile of v1, /device:TPU:1, one launch (start us, length us, event | category | flops | bytes accessed | tf_op | source)
XLA Modules:
  0.0 873.5 jit_solution(9107597892418527830)
XLA Ops:
  0.0 11.4 %copy.46 = bf16[64,16,4096]{2,0,1:T(8,128)(2,1)} copy(bf16[64,16,4096]{2,1,0:T(8,128)(2,1)} %param.3) | data formatting | bytes 16777216 | tf_op args[0]
  11.4 7.4 slice.19
  29.9 6.8 copy.54
  37.6 21.5 %mul.180 = f32[2048,64,16]{2,1,0:T(8,128)} broadcast(f32[2048,64]{1,0:T(8,128)S(1)} %copy.56), dimensions={0,1} | broadcast | bytes 8912896 | tf_op jit(solution)/shard_map/mul | solution.py:72
  59.1 54.5 %mul.181 = f32[128,16,1024]{2,1,0:T(8,128)} reshape(f32[2048,64,16]{2,1,0:T(8,128)} %mul.180) | data formatting | bytes 16777216 | tf_op jit(solution)/shard_map/mul | solution.py:72
  114.3 22.0 %fusion.3 = f32[64,16,4096]{2,0,1:T(8,128)S(1)} fusion(bf16[64,16,4096]{2,0,1:T(8,128)(2,1)} %copy.46, bf16[64,15,4096]{2,0,1:T(8,128)(2,1)} %collective-permute-done, f32[16,1,4096]{2,0,1:T(8,128)S(1)} %bitcast.69), kind=kOutput, calls=%fused_computation.6 | convolution fusion | flops 813432832 | bytes 33292288 | tf_op jit(solution)/shard_map/conv_general_dilated | solution.py:60
  136.4 18.8 %copy.49 = f32[64,16,4096]{2,1,0:T(8,128)} copy(f32[64,16,4096]{2,0,1:T(8,128)S(1)} %fusion.3) | data formatting | bytes 33554432 | tf_op jit(solution)/shard_map/conv_general_dilated | solution.py:60
  155.2 27.0 %reshape.234 = f32[1024,64,64]{2,1,0:T(8,128)} reshape(f32[64,16,4096]{2,1,0:T(8,128)} %copy.49) | data formatting | bytes 33554432 | tf_op jit(solution)/shard_map/reshape | solution.py:26
  182.2 26.2 %copy.69 = f32[1024,64,64,1]{0,1,3,2:T(8,128)} copy(f32[1024,64,64,1]{2,1,0,3:T(8,128)} %bitcast.62) | data formatting | bytes 33554432 | tf_op jit(solution)/shard_map/reshape | solution.py:26
  208.5 33.7 %convolution_bitcast_fusion = f32[2,64,64,1024,1]{3,1,0,2,4:T(8,128)} fusion(f32[1024,64,64,1]{0,1,3,2:T(8,128)} %copy.69, f32[1,64,64]{2,1,0:T(8,128)S(1)} %copy-done.5, f32[1,64,64]{2,1,0:T(8,128)S(1)} %copy-done.6), kind=kOutput, calls=%fused_computation.10 | convolution fusion | flops 6442459136 | bytes 50364416 | tf_op jit(solution)/shard_map/qka,Rab->qkbR/dot_general | solution.py:31
  242.2 47.6 %fusion.7 = f32[2,32,64,1024]{3,1,0,2:T(8,128)} fusion(f32[2,32,64,2,64]{4,1,3,0,2:T(8,128)S(1)} %copy-done.1, f32[2,64,64,1024,1]{3,1,0,2,4:T(8,128)} %convolution_bitcast_fusion), kind=kOutput, calls=%fused_computation.11 | convolution fusion | flops 6442450944 | bytes 52428800 | tf_op jit(solution)/shard_map/qjksb,skbR->qjkR/dot_general | solution.py:43
  289.7 15.6 %copy.55 = f32[2,32,64,1024]{3,2,1,0:T(8,128)S(1)} copy(f32[2,32,64,1024]{3,1,0,2:T(8,128)} %fusion.7) | data formatting | bytes 33554432 | tf_op jit(solution)/shard_map/qjksb,skbR->qjkR/transpose | solution.py:43
  310.5 8.5 copy.57
  319.1 10.1 %all-to-all-start = ((bf16[2,128,16,1024]{3,2,0,1:T(8,128)(2,1)}), bf16[2,128,16,1024]{3,2,0,1:T(8,128)(2,1)}, u32[]{:S(2)}, u32[]{:S(2)}) async-start(bf16[2,128,16,1024]{3,2,0,1:T(8,128)(2,1)} %copy.57), calls=%async_computation | async-start | bytes 16777216 | tf_op jit(solution)/shard_map/all_to_all | solution.py:75
  330.6 100.1 %all-to-all-done = bf16[2,128,16,1024]{3,2,0,1:T(8,128)(2,1)} async-done(((bf16[2,128,16,1024]{3,2,0,1:T(8,128)(2,1)}), bf16[2,128,16,1024]{3,2,0,1:T(8,128)(2,1)}, u32[]{:S(2)}, u32[]{:S(2)}) %all-to-all-start) | async-done | bytes 8388640 | tf_op jit(solution)/shard_map/all_to_all | solution.py:75
  430.6 62.1 %reshape.251 = bf16[2,8,16,16,64,16]{5,4,3,0,2,1:T(8,128)(2,1)} reshape(bf16[2,128,16,1024]{3,2,0,1:T(8,128)(2,1)} %all-to-all-done) | data formatting | bytes 16777216 | tf_op jit(solution)/shard_map/reshape | solution.py:76
  492.7 56.9 %copy.59 = bf16[2,8,16,16,64,16]{4,5,2,1,3,0:T(8,128)(2,1)} copy(bf16[2,8,16,16,64,16]{5,4,3,0,2,1:T(8,128)(2,1)} %reshape.251) | data formatting | bytes 16777216 | tf_op jit(solution)/shard_map/reshape | solution.py:76
  549.6 57.9 %copy.60 = bf16[2,16,8,64,16,16]{3,2,5,4,1,0:T(8,128)(2,1)} copy(bf16[2,16,8,64,16,16]{5,3,1,0,4,2:T(8,128)(2,1)} %bitcast.18) | data formatting | bytes 16777216 | tf_op jit(solution)/shard_map/transpose | solution.py:77
  607.5 22.5 %reshape.236 = bf16[2,16,512,256]{2,3,1,0:T(8,128)(2,1)} reshape(bf16[2,16,8,64,16,16]{3,2,5,4,1,0:T(8,128)(2,1)} %copy.60) | data formatting | bytes 16777216 | tf_op jit(solution)/shard_map/reshape | solution.py:77
  630.0 16.5 %convolution_bitcast_fusion.1 = f32[16,512,512]{2,1,0:T(8,128)} fusion(bf16[2,16,512,256]{2,3,1,0:T(8,128)(2,1)} %reshape.236), kind=kOutput, calls=%fused_computation.12 | convolution fusion | flops 4294967296 | bytes 25165824 | tf_op jit(solution)/shard_map/rcnt,rcmt->cnm/dot_general | solution.py:81
  646.4 11.7 %fusion.44 = (bf16[1,16,8,64,16,16]{3,5,4,2,1,0:T(8,128)(2,1)}, bf16[1,16,8,64,16,16]{3,5,4,2,1,0:T(8,128)(2,1)}) fusion(bf16[2,16,8,64,16,16]{3,5,4,2,1,0:T(8,128)(2,1)} %bitcast.63), kind=kLoop, calls=%fused_computation.70 | loop fusion | flops 2097152 | bytes 16777216 | tf_op jit(solution)/shard_map/slice | solution.py:80
  658.2 20.2 %copy.64 = bf16[1,16,8,64,16,16]{3,2,5,4,1,0:T(8,128)(2,1)} copy(bf16[1,16,8,64,16,16]{3,5,4,2,1,0:T(8,128)(2,1)} %get-tuple-element.6) | data formatting | bytes 8388608 | tf_op jit(solution)/shard_map/neg | solution.py:80
  678.4 11.8 %neg.47 = bf16[1,16,512,256]{2,3,1,0:T(8,128)(2,1)} reshape(bf16[1,16,8,64,16,16]{3,2,5,4,1,0:T(8,128)(2,1)} %copy.64) | data formatting | bytes 8388608 | tf_op jit(solution)/shard_map/neg | solution.py:80
  690.2 6.3 copy.66
  696.5 20.2 %copy.63 = bf16[1,16,8,64,16,16]{3,2,5,4,1,0:T(8,128)(2,1)} copy(bf16[1,16,8,64,16,16]{3,5,4,2,1,0:T(8,128)(2,1)} %get-tuple-element.5) | data formatting | bytes 8388608 | tf_op jit(solution)/shard_map/slice | solution.py:80
  716.8 11.8 %slice.15 = bf16[1,16,512,256]{2,3,1,0:T(8,128)(2,1)} reshape(bf16[1,16,8,64,16,16]{3,2,5,4,1,0:T(8,128)(2,1)} %copy.63) | data formatting | bytes 8388608 | tf_op jit(solution)/shard_map/slice | solution.py:80
  728.6 6.3 copy.65
  734.9 61.6 %copy.68 = f32[16,512,512]{0,2,1:T(8,128)} copy(f32[16,512,512]{2,1,0:T(8,128)} %convolution_bitcast_fusion.1) | data formatting | bytes 33554432 | tf_op jit(solution)/shard_map/rcnt,rcmt->cnm/dot_general | solution.py:81
  796.4 5.5 gather_fusion
  802.1 21.9 %psum.14 = f32[512]{0:T(512)S(1)} all-reduce(f32[512]{0:T(512)S(1)} %reduce_sum.9), channel_id=1, replica_groups=mesh['stn'=8,'tm'=16] {'stn'}, use_global_device_ids=true, to_apply=%region_1.2 | all-reduce | flops 512 | bytes 4096 | tf_op jit(solution)/shard_map/psum | solution.py:84
  824.0 30.0 %psum.15 = f32[512]{0:T(512)S(1)} all-reduce(f32[512]{0:T(512)S(1)} %psum.14), channel_id=1, replica_groups=mesh['stn'=8,'tm'=16] {'tm'}, use_global_device_ids=true, to_apply=%region_2.3 | all-reduce | flops 512 | bytes 4096 | tf_op jit(solution)/shard_map/psum | solution.py:84
  854.2 18.9 %fusion.2 = f32[16,512,512]{2,1,0:T(8,128)} fusion(f32[16,512,512]{2,1,0:T(8,128)} %convolution_bitcast_fusion.1, bf16[1,16,512,256]{3,2,0,1:T(8,128)(2,1)} %copy.66, bf16[1,16,512,256]{3,2,0,1:T(8,128)(2,1)} %copy.65, bf16[2,16,512,256]{2,3,1,0:T(8,128)(2,1)} %reshape.236, f32[512,512]{1,0:T(8,128)S(1)} %multiply_multiply_fusion, ...), kind=kOutput, calls=%fused_computation.4 | convolution fusion | flops 4307550208 | bytes 51642368 | tf_op jit(solution)/shard_map/rcnt,rcmt->cnm/dot_general | solution.py:82
  (41 shorter events, 19.5 us)
Async XLA Ops:
  18.8 18.0 %copy-start.4 = (f32[16,4096]{1,0:T(8,128)S(1)}, f32[16,4096]{1,0:T(8,128)}, u32[]{:S(2)}) copy-start(f32[16,4096]{1,0:T(8,128)} %param.4) | copy-start | bytes 786436
  18.8 18.5 %copy-start.3 = (f32[64,2048]{1,0:T(8,128)S(1)}, f32[64,2048]{1,0:T(8,128)}, u32[]{:S(2)}) copy-start(f32[64,2048]{1,0:T(8,128)} %param.5) | copy-start | bytes 1572868
  18.8 95.6 %collective-permute-start = (bf16[64,15,4096]{2,0,1:T(8,128)(2,1)}, bf16[64,15,4096]{2,0,1:T(8,128)(2,1)}, u32[]{:S(2)}, u32[]{:S(2)}) collective-permute-start(bf16[64,15,4096]{2,0,1:T(8,128)(2,1)} %slice.19), channel_id=1, source_target_pairs={{0,1},{1,2},{2,3},{3,4},{4,5},{5,6},{6,7},{7,8},{8,9},{9,10},{10,1... | collective-permute-start | bytes 23592968 | tf_op jit(solution)/shard_map/ppermute | solution.py:11
  182.2 26.2 %copy-start.5 = (f32[1,64,64]{2,1,0:T(8,128)S(1)}, f32[1,64,64]{2,1,0:T(8,128)}, u32[]{:S(2)}) copy-start(f32[1,64,64]{2,1,0:T(8,128)} %get-tuple-element.15) | copy-start | bytes 49156
  182.2 26.2 %copy-start.6 = (f32[1,64,64]{2,1,0:T(8,128)S(1)}, f32[1,64,64]{2,1,0:T(8,128)}, u32[]{:S(2)}) copy-start(f32[1,64,64]{2,1,0:T(8,128)} %get-tuple-element.16) | copy-start | bytes 49156
  208.5 33.7 %copy-start.1 = (f32[2,32,64,2,64]{4,1,3,0,2:T(8,128)S(1)}, f32[2,32,64,2,64]{4,1,3,0,2:T(8,128)}, u32[]{:S(2)}) copy-start(f32[2,32,64,2,64]{4,1,3,0,2:T(8,128)} %copy.54) | copy-start | bytes 6291460
  208.5 96.9 %slice-start = ((s8[8388608]{0:T(1024)(128)(4,1)}), s8[4194304]{0:T(1024)(128)(4,1)S(1)}, s32[]{:S(2)}) async-start(s8[8388608]{0:T(1024)(128)(4,1)} %bitcast.66), calls=%async_computation.1 | async-start | bytes 8388608
  242.2 63.2 %slice-start.1 = ((s8[8388608]{0:T(1024)(128)(4,1)}), s8[4194304]{0:T(1024)(128)(4,1)S(1)}, s32[]{:S(2)}) async-start(s8[8388608]{0:T(1024)(128)(4,1)} %bitcast.66), calls=%async_computation.2 | async-start | bytes 8388608
  319.1 111.6 %all-to-all-start = ((bf16[2,128,16,1024]{3,2,0,1:T(8,128)(2,1)}), bf16[2,128,16,1024]{3,2,0,1:T(8,128)(2,1)}, u32[]{:S(2)}, u32[]{:S(2)}) async-start(bf16[2,128,16,1024]{3,2,0,1:T(8,128)(2,1)} %copy.57), calls=%async_computation | async-start | bytes 16777216 | tf_op jit(solution)/shard_map/all_to_all | solution.py:75
  734.9 61.6 %copy-start = (s32[512,1]{0,1:T(1,128)S(1)}, s32[512,1]{0,1:T(1,128)}, u32[]{:S(2)}) copy-start(s32[512,1]{0,1:T(1,128)} %shift-left_or_fusion) | copy-start | bytes 6148
  734.9 119.3 %copy-start.2 = (pred[512,512]{1,0:T(8,128)(4,1)S(1)}, pred[512,512]{1,0:T(8,128)(4,1)}, u32[]{:S(2)}) copy-start(pred[512,512]{1,0:T(8,128)(4,1)} %iota_compare_fusion) | copy-start | bytes 786436
